TPU v7x, 32 devices: a whole 2x2x4 slice. The times are simulated.
32 devices in a mesh: outer: 4 (over y, x), inner: 8 (over z, core).
Axes of the slice: x: 2, y: 2, z: 4, core: 2. Of those that a mesh axis runs over, the one named last changes fastest.
Arguments:
- queries: bfloat16 [8192, 1024], P(('outer', 'inner')), may hold values from -480 to 480
- keys: bfloat16 [8192, 512], P(('outer', 'inner')), may hold values from -8 to 8
- values: bfloat16 [8192, 512], P(('outer', 'inner')), may hold values from -4 to 4
- residual: bfloat16 [8192, 1024], P(('outer', 'inner')), may hold values from -5 to 5
- norm_gain: float32 [1024], replicated, may hold values from 0.1 to 1.9
- w_gate: bfloat16 [8, 1024, 512], P('inner'), may hold values from -0.1875 to 0.1875
- w_up: bfloat16 [8, 1024, 512], P('inner'), may hold values from -0.1875 to 0.1875
- w_down: bfloat16 [8, 512, 1024], P('inner'), may hold values from -0.25 to 0.25
- routes: int32 [8192, 2], P(('outer', 'inner')), may hold values from 0 to 7, all different within a row; in each aligned block of 256 rows (0 to 255, 256 to 511, ...) at most 128 rows name the same one
- gates: float32 [8192, 2], P(('outer', 'inner')), may hold values from 0.2 to 1
Outputs:
- layer_out: bfloat16 [8192, 1024], P(('outer', 'inner'))
Inputs may be any that keep to these rules, and one draw needn't show every extreme that they name: `routes`: A patch's two experts differ. Within one block of 256 patches no expert is picked more than 128 times, and in some block one expert is picked exactly 128 times.
All inputs are finite; a program needn't handle non-finite values.
Results may differ from a plain program's by a relative error of at most 0.0085.
Values may be sent and summed in bfloat16 or wider, within the bound.
A program may use at most 64 MiB of HBM per device.

v0:
```python
import math
import jax
import jax.numpy as jnp
from jax import lax
from jax.sharding import PartitionSpec as P

D = 1024
QH = 8
KVH = 4
DH = 128
BACK = 3


def shifted(value, axis, steps):
    count = lax.axis_size(axis)
    first, last = (max(0, -steps), min(count, count - steps))
    return lax.ppermute(value, axis, [(source, source + steps) for source in range(first, last)])


def feed_forward(rows, gate_matrix, up_matrix, down_matrix):
    gate_part = jnp.dot(rows, gate_matrix, preferred_element_type=jnp.float32)
    up_part = jnp.dot(rows, up_matrix, preferred_element_type=jnp.float32)
    inner_act = (jax.nn.silu(gate_part) * up_part).astype(jnp.bfloat16)
    return jnp.dot(inner_act, down_matrix, preferred_element_type=jnp.float32).astype(jnp.bfloat16)


def local(queries, keys, values, residual, norm_gain, w_gate, w_up, w_down, routes, gates):
    tok_rows = queries.shape[0]
    groups = QH // KVH
    device_index = lax.axis_index(("outer", "inner"))
    current = (keys, values)
    earlier = []
    for step_index in range(BACK):
        current = shifted((current[0], current[1]), ("outer", "inner"), 1)
        earlier = [current] + earlier
    key_window = jnp.concatenate([block_pair[0] for block_pair in earlier] + [keys], 0)
    value_window = jnp.concatenate([block_pair[1] for block_pair in earlier] + [values], 0)
    window_rows = key_window.shape[0]
    query_heads = queries.reshape(tok_rows, KVH, groups, DH)
    key_heads = key_window.reshape(window_rows, KVH, DH)
    value_heads = value_window.reshape(window_rows, KVH, DH)
    scores = jnp.einsum(
        "tkgd,skd->kgts", query_heads, key_heads, preferred_element_type=jnp.float32
    ) * (1.0 / math.sqrt(DH))
    query_pos = device_index * tok_rows + jnp.arange(tok_rows, dtype=jnp.int32)
    key_pos = (device_index - BACK) * tok_rows + jnp.arange(window_rows, dtype=jnp.int32)
    allowed = (key_pos[None, :] >= 0) & (key_pos[None, :] <= query_pos[:, None])
    scores = jnp.where(allowed, scores, -jnp.inf)
    highest = jnp.max(scores, -1, keepdims=True)
    expd = jnp.exp(scores - highest)
    weights = (expd / jnp.sum(expd, -1, keepdims=True)).astype(jnp.bfloat16)
    mixed = jnp.einsum("kgts,skd->tkgd", weights, value_heads, preferred_element_type=jnp.float32)
    attended = mixed.astype(jnp.bfloat16).reshape(tok_rows, QH * DH)
    stream = residual.astype(jnp.float32) + attended.astype(jnp.float32)
    mean_sq = jnp.mean(stream * stream, -1, keepdims=True)
    normed = (stream * lax.rsqrt(mean_sq + 1e-06) * norm_gain).astype(jnp.bfloat16)
    owners = lax.axis_size("inner")
    capacity = 4 * tok_rows // owners
    picks = routes.reshape(-1)
    one_hot = (picks[:, None] == jnp.arange(owners, dtype=jnp.int32)[None, :]).astype(jnp.int32)
    order_rank = jnp.sum((jnp.cumsum(one_hot, 0) - 1) * one_hot, 1)
    slot_index = picks * capacity + order_rank
    slot_pair = slot_index.reshape(tok_rows, 2)
    slot_grid = jnp.arange(owners * capacity, dtype=jnp.int32)[:, None]
    placing = ((slot_pair[None, :, 0] == slot_grid) | (slot_pair[None, :, 1] == slot_grid)).astype(
        jnp.bfloat16
    )
    outgoing = (
        jnp.dot(placing, normed, preferred_element_type=jnp.float32)
        .astype(jnp.bfloat16)
        .reshape(owners, capacity, D)
    )
    gate_matrix = w_gate[0]
    up_matrix = w_up[0]
    down_matrix = w_down[0]
    arrived = lax.all_to_all(outgoing, "inner", split_axis=0, concat_axis=0, tiled=True)
    results = feed_forward(arrived.reshape(-1, D), gate_matrix, up_matrix, down_matrix).reshape(
        arrived.shape
    )
    returned = lax.all_to_all(results, "inner", split_axis=0, concat_axis=0, tiled=True)
    picked = (
        returned.reshape(owners * capacity, D)[slot_index]
        .astype(jnp.float32)
        .reshape(tok_rows, 2, D)
    )
    mixture = jnp.sum(gates[:, :, None] * picked, 1)
    return (stream + mixture).astype(jnp.bfloat16)


def solution(mesh):
    return jax.shard_map(
        local,
        mesh=mesh,
        in_specs=(
            P(("outer", "inner"), None),
            P(("outer", "inner"), None),
            P(("outer", "inner"), None),
            P(("outer", "inner"), None),
            P(),
            P("inner", None, None),
            P("inner", None, None),
            P("inner", None, None),
            P(("outer", "inner"), None),
            P(("outer", "inner"), None),
        ),
        out_specs=P(("outer", "inner"), None),
        check_vma=False,
    )
```

profile of v0, /device:TPU:4, one launch (start us, length us, event | category | flops | bytes accessed | tf_op | source)
XLA Modules:
  0.0 177.8 jit_solution(39388173408413153)
XLA Ops:
  0.0 0.0 copy-start
  0.0 0.0 copy-start.5
  0.0 1.2 copy.28
  1.2 1.9 %collective-permute-start.3 = (bf16[256,512]{0,1:T(8,128)(2,1)S(1)}, bf16[256,512]{0,1:T(8,128)(2,1)S(1)}, u32[]{:S(2)}, u32[]{:S(2)}) collective-permute-start(bf16[256,512]{0,1:T(8,128)(2,1)S(1)} %copy.28), channel_id=1, source_target_pairs={{0,1},{1,2},{2,3},{3,4},{4,5},{5,6},{6,7},{7,8},{8,9},{9,10},{10,1... | collective-permute-start | bytes 786440 | tf_op jit(solution)/shard_map/ppermute | solution.py:17
  3.1 3.6 %collective-permute-start = (bf16[256,512]{1,0:T(8,128)(2,1)}, bf16[256,512]{1,0:T(8,128)(2,1)S(1)}, u32[]{:S(2)}, u32[]{:S(2)}) collective-permute-start(bf16[256,512]{1,0:T(8,128)(2,1)} %param.12), channel_id=1, source_target_pairs={{0,1},{1,2},{2,3},{3,4},{4,5},{5,6},{6,7},{7,8},{8,9},{9,10},{10,1... | collective-permute-start | bytes 786440 | tf_op jit(solution)/shard_map/ppermute | solution.py:17
  6.7 0.8 copy.35
  7.6 0.1 eq.59
  7.7 1.1 reduce-window.6
  8.9 0.2 slice_reduce_fusion.2
  9.1 0.1 eq.55
  9.3 0.1 fusion.29
  9.4 3.1 %collective-permute-done.3 = bf16[256,512]{0,1:T(8,128)(2,1)S(1)} collective-permute-done((bf16[256,512]{0,1:T(8,128)(2,1)S(1)}, bf16[256,512]{0,1:T(8,128)(2,1)S(1)}, u32[]{:S(2)}, u32[]{:S(2)}) %collective-permute-start.3) | collective-permute-done | bytes 262176 | tf_op jit(solution)/shard_map/ppermute | solution.py:17
  12.5 0.0 copy-start.6
  12.5 1.9 %collective-permute-start.4 = (bf16[256,512]{0,1:T(8,128)(2,1)S(1)}, bf16[256,512]{0,1:T(8,128)(2,1)}, u32[]{:S(2)}, u32[]{:S(2)}) collective-permute-start(bf16[256,512]{0,1:T(8,128)(2,1)S(1)} %collective-permute-done.3), channel_id=1, source_target_pairs={{0,1},{1,2},{2,3},{3,4},{4,5},{5,6},{6,7},{7,8},{8,9},{9,10},{10,1... | collective-permute-start | bytes 786440 | tf_op jit(solution)/shard_map/ppermute | solution.py:17
  14.4 0.9 collective-permute-done
  15.3 0.0 copy-start.7
  15.3 1.9 %collective-permute-start.1 = (bf16[256,512]{1,0:T(8,128)(2,1)S(1)}, bf16[256,512]{1,0:T(8,128)(2,1)S(1)}, u32[]{:S(2)}, u32[]{:S(2)}) collective-permute-start(bf16[256,512]{1,0:T(8,128)(2,1)S(1)} %collective-permute-done), channel_id=1, source_target_pairs={{0,1},{1,2},{2,3},{3,4},{4,5},{5,6},{6,7},{7,8},{8,9},{9,10},{10,1... | collective-permute-start | bytes 786440 | tf_op jit(solution)/shard_map/ppermute | solution.py:17
  17.2 0.1 reduce_sum.42
  17.4 6.5 %collective-permute-done.4 = bf16[256,512]{0,1:T(8,128)(2,1)} collective-permute-done((bf16[256,512]{0,1:T(8,128)(2,1)S(1)}, bf16[256,512]{0,1:T(8,128)(2,1)}, u32[]{:S(2)}, u32[]{:S(2)}) %collective-permute-start.4) | collective-permute-done | bytes 262176 | tf_op jit(solution)/shard_map/ppermute | solution.py:17
  23.9 1.9 %collective-permute-start.5 = (bf16[256,512]{0,1:T(8,128)(2,1)}, bf16[256,512]{0,1:T(8,128)(2,1)}, u32[]{:S(2)}, u32[]{:S(2)}) collective-permute-start(bf16[256,512]{0,1:T(8,128)(2,1)} %collective-permute-done.4), channel_id=1, source_target_pairs={{0,1},{1,2},{2,3},{3,4},{4,5},{5,6},{6,7},{7,8},{8,9},{9,10},{10,1... | collective-permute-start | bytes 786440 | tf_op jit(solution)/shard_map/ppermute | solution.py:17
  25.8 0.8 collective-permute-done.1
  26.6 0.0 copy-start.8
  26.6 1.9 %collective-permute-start.2 = (bf16[256,512]{1,0:T(8,128)(2,1)S(1)}, bf16[256,512]{1,0:T(8,128)(2,1)}, u32[]{:S(2)}, u32[]{:S(2)}) collective-permute-start(bf16[256,512]{1,0:T(8,128)(2,1)S(1)} %collective-permute-done.1), channel_id=1, source_target_pairs={{0,1},{1,2},{2,3},{3,4},{4,5},{5,6},{6,7},{7,8},{8,9},{9,10},{10,1... | collective-permute-start | bytes 786440 | tf_op jit(solution)/shard_map/ppermute | solution.py:17
  28.5 1.1 compare_and_fusion
  29.6 0.0 copy-done.5
  29.6 1.2 reshape.106
  30.7 0.2 slice_reduce_fusion.1
  30.9 0.0 copy-done.6
  30.9 0.0 copy-done.7
  30.9 0.0 copy-done.8
  30.9 7.3 %collective-permute-done.2 = bf16[256,512]{1,0:T(8,128)(2,1)} collective-permute-done((bf16[256,512]{1,0:T(8,128)(2,1)S(1)}, bf16[256,512]{1,0:T(8,128)(2,1)}, u32[]{:S(2)}, u32[]{:S(2)}) %collective-permute-start.2) | collective-permute-done | bytes 262176 | tf_op jit(solution)/shard_map/ppermute | solution.py:17
  38.3 1.3 pad_maximum_fusion
  39.5 0.5 copy.27
  40.1 0.0 collective-permute-done.5
  40.1 1.2 pad_maximum_fusion.1
  41.3 7.1 %fusion.35 = (f32[4,2,256]{2,1,0:T(2,128)S(1)}, f32[4,2,256,1024]{2,3,1,0:T(8,128)}) fusion(pred[256,1024]{0,1:T(8,128)(4,1)} %compare_and_fusion, bf16[1024,4,128,1]{0,2,3,1:T(8,128)(2,1)S(1)} %bitcast.57, bf16[256,4,2,128]{3,2,1,0:T(2,128)(2,1)} %reshape.106), kind=kOutput, calls=%fused_computation.58 | convolution fusion | flops 545260544 | bytes 10231808 | tf_op jit(solution)/shard_map/sub | solution.py:50
  48.5 5.2 %fusion.7 = f32[4,128,2,256]{3,1,2,0:T(8,128)} fusion(bf16[1024,4,128,1]{0,2,3,1:T(8,128)(2,1)S(1)} %bitcast.56, f32[4,2,256,1024]{2,3,1,0:T(8,128)} %get-tuple-element.10, f32[4,2,256]{2,1,0:T(2,128)S(1)} %get-tuple-element.9), kind=kOutput, calls=%fused_computation.15 | convolution fusion | flops 541589504 | bytes 10493952 | tf_op jit(solution)/shard_map/kgts,skd->tkgd/dot_general | solution.py:52
  53.6 0.0 copy-start.3
  53.6 1.6 copy.33
  55.3 0.0 copy-done.3
  55.3 0.0 copy-start.1
  55.3 0.2 multiply_reduce_fusion.1
  55.5 0.0 copy-done.9
  55.5 0.8 convolution_convert_fusion.1
  56.4 0.0 copy-done.1
  56.4 0.0 copy-start.11
  56.4 51.6 %all_to_all.10 = bf16[8,128,1024]{2,1,0:T(8,128)(2,1)S(1)} all-to-all(bf16[8,128,1024]{2,1,0:T(8,128)(2,1)S(1)} %bitcast.52), channel_id=1, replica_groups=mesh['outer'=4,'inner'=8] {'inner'}, dimensions={0} | all-to-all | bytes 4194304 | tf_op jit(solution)/shard_map/all_to_all | solution.py:76
  108.0 0.0 copy-done.11
  108.0 2.6 %fusion.11 = f32[1024,512]{1,0:T(8,128)} fusion(bf16[1024,1024]{1,0:T(8,128)(2,1)S(1)} %bitcast.54, bf16[1,1024,512]{2,1,0:T(8,128)(2,1)S(1)} %copy-done.11), kind=kOutput, calls=%fused_computation.20 | convolution fusion | flops 1073741824 | bytes 5242880 | tf_op jit(solution)/shard_map/dot_general | solution.py:21
  110.6 0.0 copy-done
  110.6 5.6 %convolution_convert_fusion = bf16[1024,1024]{1,0:T(8,128)(2,1)} fusion(f32[1024,512]{1,0:T(8,128)} %fusion.11, bf16[1024,1024]{1,0:T(8,128)(2,1)S(1)} %bitcast.55, bf16[1,512,1024]{2,1,0:T(8,128)(2,1)S(1)} %copy-done, bf16[1,1024,512]{2,1,0:T(8,128)(2,1)} %param.16), kind=kOutput, calls=%fused_computation.12 | convolution fusion | flops 2151677952 | bytes 8388608 | tf_op jit(solution)/shard_map/dot_general | solution.py:24
  116.2 3.9 %all-to-all-start.1 = ((bf16[8,128,1024]{2,1,0:T(8,128)(2,1)}), bf16[8,128,1024]{2,1,0:T(8,128)(2,1)S(1)}, u32[]{:S(2)}, u32[]{:S(2)}) async-start(bf16[8,128,1024]{2,1,0:T(8,128)(2,1)} %bitcast.53), calls=%async_computation.1 | async-start | bytes 4194304 | tf_op jit(solution)/shard_map/all_to_all | solution.py:80
  120.1 0.1 mul.89
  120.3 0.0 copy-done.10
  120.3 0.1 copy.34
  120.5 48.5 %all-to-all-done.1 = bf16[8,128,1024]{2,1,0:T(8,128)(2,1)S(1)} async-done(((bf16[8,128,1024]{2,1,0:T(8,128)(2,1)}), bf16[8,128,1024]{2,1,0:T(8,128)(2,1)S(1)}, u32[]{:S(2)}, u32[]{:S(2)}) %all-to-all-start.1) | async-done | bytes 2097184 | tf_op jit(solution)/shard_map/all_to_all | solution.py:80
  168.9 2.8 %gather_fusion = bf16[512,1024]{1,0:T(8,128)(2,1)} fusion(bf16[1024,1024]{1,0:T(8,128)(2,1)S(1)} %bitcast.51, s32[1024]{0:T(1024)S(1)} %pad_clamp_fusion), kind=kCustom, calls=%fused_computation | custom fusion | bytes 2099200 | tf_op jit(solution)/shard_map/gather | solution.py:82
  171.7 2.4 %reshape.113 = f32[256,2,1024]{2,1,0:T(2,128)S(1)} reshape(bf16[512,1024]{1,0:T(8,128)(2,1)} %gather_fusion) | data formatting | bytes 3145728 | tf_op jit(solution)/shard_map/convert_element_type | solution.py:83
  174.1 0.0 copy-start.2
  174.1 0.0 copy-start.4
  174.1 2.6 %multiply_reduce_fusion = f32[256,1024]{1,0:T(8,128)S(1)} fusion(f32[256,2,1024]{2,1,0:T(2,128)S(1)} %reshape.113, f32[256,2]{1,0:T(8,128)S(1)} %copy.34), kind=kLoop, calls=%fused_computation.10 | loop fusion | flops 786432 | bytes 3147776 | tf_op jit(solution)/shard_map/reduce_sum | solution.py:86
  176.8 0.0 copy-done.2
  176.8 0.0 copy-done.4
  176.8 1.1 add_convert_fusion
  (12 shorter events, 0.1 us)
Async XLA Ops:
  0.0 110.6 %copy-start = (bf16[1,512,1024]{2,1,0:T(8,128)(2,1)S(1)}, bf16[1,512,1024]{2,1,0:T(8,128)(2,1)}, u32[]{:S(2)}) copy-start(bf16[1,512,1024]{2,1,0:T(8,128)(2,1)} %param.17) | copy-start | bytes 3145732
  0.0 29.6 %copy-start.5 = (bf16[256,1024]{1,0:T(8,128)(2,1)S(1)}, bf16[256,1024]{1,0:T(8,128)(2,1)}, u32[]{:S(2)}) copy-start(bf16[256,1024]{1,0:T(8,128)(2,1)} %param.10) | copy-start | bytes 1572868
  1.2 11.3 %collective-permute-start.3 = (bf16[256,512]{0,1:T(8,128)(2,1)S(1)}, bf16[256,512]{0,1:T(8,128)(2,1)S(1)}, u32[]{:S(2)}, u32[]{:S(2)}) collective-permute-start(bf16[256,512]{0,1:T(8,128)(2,1)S(1)} %copy.28), channel_id=1, source_target_pairs={{0,1},{1,2},{2,3},{3,4},{4,5},{5,6},{6,7},{7,8},{8,9},{9,10},{10,1... | collective-permute-start | bytes 786440 | tf_op jit(solution)/shard_map/ppermute | solution.py:17
  3.1 12.2 %collective-permute-start = (bf16[256,512]{1,0:T(8,128)(2,1)}, bf16[256,512]{1,0:T(8,128)(2,1)S(1)}, u32[]{:S(2)}, u32[]{:S(2)}) collective-permute-start(bf16[256,512]{1,0:T(8,128)(2,1)} %param.12), channel_id=1, source_target_pairs={{0,1},{1,2},{2,3},{3,4},{4,5},{5,6},{6,7},{7,8},{8,9},{9,10},{10,1... | collective-permute-start | bytes 786440 | tf_op jit(solution)/shard_map/ppermute | solution.py:17
  12.5 18.4 %copy-start.6 = (bf16[256,512]{0,1:T(8,128)(2,1)}, bf16[256,512]{0,1:T(8,128)(2,1)S(1)}, u32[]{:S(2)}) copy-start(bf16[256,512]{0,1:T(8,128)(2,1)S(1)} %collective-permute-done.3) | copy-start | bytes 786436
  12.5 11.4 %collective-permute-start.4 = (bf16[256,512]{0,1:T(8,128)(2,1)S(1)}, bf16[256,512]{0,1:T(8,128)(2,1)}, u32[]{:S(2)}, u32[]{:S(2)}) collective-permute-start(bf16[256,512]{0,1:T(8,128)(2,1)S(1)} %collective-permute-done.3), channel_id=1, source_target_pairs={{0,1},{1,2},{2,3},{3,4},{4,5},{5,6},{6,7},{7,8},{8,9},{9,10},{10,1... | collective-permute-start | bytes 786440 | tf_op jit(solution)/shard_map/ppermute | solution.py:17
  15.3 15.6 %copy-start.7 = (bf16[256,512]{1,0:T(8,128)(2,1)}, bf16[256,512]{1,0:T(8,128)(2,1)S(1)}, u32[]{:S(2)}) copy-start(bf16[256,512]{1,0:T(8,128)(2,1)S(1)} %collective-permute-done) | copy-start | bytes 786436
  15.3 11.3 %collective-permute-start.1 = (bf16[256,512]{1,0:T(8,128)(2,1)S(1)}, bf16[256,512]{1,0:T(8,128)(2,1)S(1)}, u32[]{:S(2)}, u32[]{:S(2)}) collective-permute-start(bf16[256,512]{1,0:T(8,128)(2,1)S(1)} %collective-permute-done), channel_id=1, source_target_pairs={{0,1},{1,2},{2,3},{3,4},{4,5},{5,6},{6,7},{7,8},{8,9},{9,10},{10,1... | collective-permute-start | bytes 786440 | tf_op jit(solution)/shard_map/ppermute | solution.py:17
  23.9 16.2 %collective-permute-start.5 = (bf16[256,512]{0,1:T(8,128)(2,1)}, bf16[256,512]{0,1:T(8,128)(2,1)}, u32[]{:S(2)}, u32[]{:S(2)}) collective-permute-start(bf16[256,512]{0,1:T(8,128)(2,1)} %collective-permute-done.4), channel_id=1, source_target_pairs={{0,1},{1,2},{2,3},{3,4},{4,5},{5,6},{6,7},{7,8},{8,9},{9,10},{10,1... | collective-permute-start | bytes 786440 | tf_op jit(solution)/shard_map/ppermute | solution.py:17
  26.6 4.4 %copy-start.8 = (bf16[256,512]{1,0:T(8,128)(2,1)}, bf16[256,512]{1,0:T(8,128)(2,1)S(1)}, u32[]{:S(2)}) copy-start(bf16[256,512]{1,0:T(8,128)(2,1)S(1)} %collective-permute-done.1) | copy-start | bytes 786436
  26.6 11.7 %collective-permute-start.2 = (bf16[256,512]{1,0:T(8,128)(2,1)S(1)}, bf16[256,512]{1,0:T(8,128)(2,1)}, u32[]{:S(2)}, u32[]{:S(2)}) collective-permute-start(bf16[256,512]{1,0:T(8,128)(2,1)S(1)} %collective-permute-done.1), channel_id=1, source_target_pairs={{0,1},{1,2},{2,3},{3,4},{4,5},{5,6},{6,7},{7,8},{8,9},{9,10},{10,1... | collective-permute-start | bytes 786440 | tf_op jit(solution)/shard_map/ppermute | solution.py:17
  53.6 1.6 copy-start.3
  53.6 1.9 %copy-start.9 = (f32[1024]{0:T(1024)S(1)}, f32[1024]{0:T(1024)}, u32[]{:S(2)}) copy-start(f32[1024]{0:T(1024)} %param.14) | copy-start | bytes 12292
  55.3 1.1 copy-start.1
  56.4 51.6 %copy-start.11 = (bf16[1,1024,512]{2,1,0:T(8,128)(2,1)S(1)}, bf16[1,1024,512]{2,1,0:T(8,128)(2,1)}, u32[]{:S(2)}) copy-start(bf16[1,1024,512]{2,1,0:T(8,128)(2,1)} %param.15) | copy-start | bytes 3145732
  116.2 4.1 %copy-start.10 = (f32[256,2]{0,1:T(2,128)S(1)}, f32[256,2]{0,1:T(2,128)}, u32[]{:S(2)}) copy-start(f32[256,2]{0,1:T(2,128)} %param.19) | copy-start | bytes 6148
  116.2 52.7 %all-to-all-start.1 = ((bf16[8,128,1024]{2,1,0:T(8,128)(2,1)}), bf16[8,128,1024]{2,1,0:T(8,128)(2,1)S(1)}, u32[]{:S(2)}, u32[]{:S(2)}) async-start(bf16[8,128,1024]{2,1,0:T(8,128)(2,1)} %bitcast.53), calls=%async_computation.1 | async-start | bytes 4194304 | tf_op jit(solution)/shard_map/all_to_all | solution.py:80
  174.1 2.7 %copy-start.2 = (f32[256,1024]{1,0:T(8,128)S(1)}, f32[256,1024]{1,0:T(8,128)}, u32[]{:S(2)}) copy-start(f32[256,1024]{1,0:T(8,128)} %copy-done.1) | copy-start | bytes 3145732
  174.1 2.7 %copy-start.4 = (bf16[256,1024]{1,0:T(8,128)(2,1)S(1)}, bf16[256,1024]{1,0:T(8,128)(2,1)}, u32[]{:S(2)}) copy-start(bf16[256,1024]{1,0:T(8,128)(2,1)} %param.13) | copy-start | bytes 1572868
where the time goes:
time: 178 us
  waiting for transfers between devices  67.1 us (38%)
  blocking collectives  51.6 us (29%)
  matrix products  21.4 us (12%)
  starting transfers between devices  17.1 us (10%)
  local copies, waits for them, and re-layouts  11.6 us (7%)
  other arithmetic  8.8 us (5%)
    all_to_all x1, blocking collectives, local(): lax.all_to_all(outgoing, 'inner', split_axis=0, concat_axis=0, tiled=True)  51.6 us
    all_to_all x1, waiting for transfers between devices, local(): lax.all_to_all(results, 'inner', split_axis=0, concat_axis=0, tiled=True)  48.5 us
    ppermute x6, waiting for transfers between devices, shifted(): lax.ppermute(value, axis, [(source, source + steps) for source in range(f...  18.6 us
    ppermute x6, starting transfers between devices, shifted(): lax.ppermute(value, axis, [(source, source + steps) for source in range(f...  13.1 us
    sub x1, matrix products, local(): expd = jnp.exp(scores - highest)  7.12 us
    dot_general x1, matrix products, feed_forward(): jnp.dot(inner_act, down_matrix, preferred_element_type=jnp.float32)  5.63 us
    dot_general x1, matrix products, local(): jnp.einsum('kgts,skd->tkgd', weights, value_heads, preferred_element_type...  5.18 us
    all_to_all x1, starting transfers between devices, local(): lax.all_to_all(results, 'inner', split_axis=0, concat_axis=0, tiled=True)  3.91 us
  transfers between devices with their start and end apart: 7, of which 6 were waited for; matrix products, arithmetic and copies ran while one was open for 4% of the time, Pallas kernels for 0%

commit v1 on v0

--- a/solution.py
+++ b/solution.py
@@ -73,7 +73,19 @@
     gate_matrix = w_gate[0]
     up_matrix = w_up[0]
     down_matrix = w_down[0]
-    arrived = lax.all_to_all(outgoing, "inner", split_axis=0, concat_axis=0, tiled=True)
+    ways, here = (lax.axis_size("inner"), lax.axis_index("inner"))
+    width = outgoing.shape[0] // ways
+    shape = list(outgoing.shape)
+    shape[0] = width
+    height = shape[0]
+    shape[0] = height * ways
+    full = jnp.zeros(shape, outgoing.dtype)
+    for mask in range(ways):
+        part = lax.dynamic_slice_in_dim(outgoing, (here ^ mask) * width, width, axis=0)
+        if mask:
+            part = lax.ppermute(part, "inner", [(d, d ^ mask) for d in range(ways)])
+        full = lax.dynamic_update_slice_in_dim(full, part, (here ^ mask) * height, axis=0)
+    arrived = full
     results = feed_forward(arrived.reshape(-1, D), gate_matrix, up_matrix, down_matrix).reshape(
         arrived.shape
     )

time: 178 us -> 176 us (0.989)
  blocking collectives: 51.6 us -> 0 us
  waiting for transfers between devices: 67.1 us -> 101 us
  starting transfers between devices: 17.1 us -> 30.9 us
    all_to_all x1 -> x0, blocking collectives: 51.6 us -> none  [local(): lax.all_to_all(outgoing, 'inner', split_axis=0, concat_axis=0, tiled=True)]
    ppermute x0 -> x7, waiting for transfers between devices: none -> 34.2 us  [local(): part = lax.ppermute(part, 'inner', [(d, d ^ mask) for d in range(ways)])]
    all_to_all x1, starting transfers between devices: 3.91 us -> 13.2 us  [local(): lax.all_to_all(results, 'inner', split_axis=0, concat_axis=0, tiled=True)]
    ppermute x0 -> x7, starting transfers between devices: none -> 4.56 us  [local(): part = lax.ppermute(part, 'inner', [(d, d ^ mask) for d in range(ways)])]
  transfers between devices with their start and end apart: 7 -> 14, of which waited for: 6 -> 10; matrix products, arithmetic and copies ran while one was open for 4% -> 4% of each run, Pallas kernels for 0% -> 0%
where the time goes in v1:
time: 176 us; the launch traced here: 175 us
  waiting for transfers between devices  101 us (57%)
  starting transfers between devices  30.9 us (18%)
  matrix products  21.3 us (12%)
  local copies, waits for them, and re-layouts  12.3 us (7%)
  other arithmetic  8.73 us (5%)
    all_to_all x1, waiting for transfers between devices, local(): lax.all_to_all(results, 'inner', split_axis=0, concat_axis=0, tiled=True)  48.7 us
    ppermute x7, waiting for transfers between devices, local(): part = lax.ppermute(part, 'inner', [(d, d ^ mask) for d in range(ways)])  34.2 us
    ppermute x6, waiting for transfers between devices, shifted(): lax.ppermute(value, axis, [(source, source + steps) for source in range(f...  18.5 us
    all_to_all x1, starting transfers between devices, local(): lax.all_to_all(results, 'inner', split_axis=0, concat_axis=0, tiled=True)  13.2 us
    ppermute x6, starting transfers between devices, shifted(): lax.ppermute(value, axis, [(source, source + steps) for source in range(f...  13.1 us
    sub x1, matrix products, local(): expd = jnp.exp(scores - highest)  7.11 us
    dot_general x1, matrix products, feed_forward(): jnp.dot(inner_act, down_matrix, preferred_element_type=jnp.float32)  5.63 us
    dot_general x1, matrix products, local(): jnp.einsum('kgts,skd->tkgd', weights, value_heads, preferred_element_type...  5.15 us
  transfers between devices with their start and end apart: 14, of which 10 were waited for; matrix products, arithmetic and copies ran while one was open for 4% of the time, Pallas kernels for 0%

profile of v1, /device:TPU:4, one launch (start us, length us, event | category | flops | bytes accessed | tf_op | source)
XLA Modules:
  0.0 175.0 jit_solution(8013081185423981744)
XLA Ops:
  0.0 0.0 copy-start
  0.0 1.2 copy.28
  1.2 1.9 %collective-permute-start.3 = (bf16[256,512]{0,1:T(8,128)(2,1)S(1)}, bf16[256,512]{0,1:T(8,128)(2,1)S(1)}, u32[]{:S(2)}, u32[]{:S(2)}) collective-permute-start(bf16[256,512]{0,1:T(8,128)(2,1)S(1)} %copy.28), channel_id=1, source_target_pairs={{0,1},{1,2},{2,3},{3,4},{4,5},{5,6},{6,7},{7,8},{8,9},{9,10},{10,1... | collective-permute-start | bytes 786440 | tf_op jit(solution)/shard_map/ppermute | solution.py:17
  3.1 3.6 %collective-permute-start = (bf16[256,512]{1,0:T(8,128)(2,1)}, bf16[256,512]{1,0:T(8,128)(2,1)S(1)}, u32[]{:S(2)}, u32[]{:S(2)}) collective-permute-start(bf16[256,512]{1,0:T(8,128)(2,1)} %param.12), channel_id=1, source_target_pairs={{0,1},{1,2},{2,3},{3,4},{4,5},{5,6},{6,7},{7,8},{8,9},{9,10},{10,1... | collective-permute-start | bytes 786440 | tf_op jit(solution)/shard_map/ppermute | solution.py:17
  6.7 0.8 copy.35
  7.6 0.1 eq.59
  7.7 1.1 reduce-window.6
  8.9 0.2 slice_reduce_fusion.2
  9.1 0.1 eq.55
  9.3 0.1 fusion.33
  9.4 3.1 %collective-permute-done.3 = bf16[256,512]{0,1:T(8,128)(2,1)S(1)} collective-permute-done((bf16[256,512]{0,1:T(8,128)(2,1)S(1)}, bf16[256,512]{0,1:T(8,128)(2,1)S(1)}, u32[]{:S(2)}, u32[]{:S(2)}) %collective-permute-start.3) | collective-permute-done | bytes 262176 | tf_op jit(solution)/shard_map/ppermute | solution.py:17
  12.5 1.9 %collective-permute-start.4 = (bf16[256,512]{0,1:T(8,128)(2,1)S(1)}, bf16[256,512]{0,1:T(8,128)(2,1)}, u32[]{:S(2)}, u32[]{:S(2)}) collective-permute-start(bf16[256,512]{0,1:T(8,128)(2,1)S(1)} %collective-permute-done.3), channel_id=1, source_target_pairs={{0,1},{1,2},{2,3},{3,4},{4,5},{5,6},{6,7},{7,8},{8,9},{9,10},{10,1... | collective-permute-start | bytes 786440 | tf_op jit(solution)/shard_map/ppermute | solution.py:17
  14.4 0.9 collective-permute-done
  15.3 1.9 %collective-permute-start.1 = (bf16[256,512]{1,0:T(8,128)(2,1)S(1)}, bf16[256,512]{1,0:T(8,128)(2,1)S(1)}, u32[]{:S(2)}, u32[]{:S(2)}) collective-permute-start(bf16[256,512]{1,0:T(8,128)(2,1)S(1)} %collective-permute-done), channel_id=1, source_target_pairs={{0,1},{1,2},{2,3},{3,4},{4,5},{5,6},{6,7},{7,8},{8,9},{9,10},{10,1... | collective-permute-start | bytes 786440 | tf_op jit(solution)/shard_map/ppermute | solution.py:17
  17.2 0.1 reduce_sum.42
  17.4 6.5 %collective-permute-done.4 = bf16[256,512]{0,1:T(8,128)(2,1)} collective-permute-done((bf16[256,512]{0,1:T(8,128)(2,1)S(1)}, bf16[256,512]{0,1:T(8,128)(2,1)}, u32[]{:S(2)}, u32[]{:S(2)}) %collective-permute-start.4) | collective-permute-done | bytes 262176 | tf_op jit(solution)/shard_map/ppermute | solution.py:17
  23.9 1.9 %collective-permute-start.5 = (bf16[256,512]{0,1:T(8,128)(2,1)}, bf16[256,512]{0,1:T(8,128)(2,1)}, u32[]{:S(2)}, u32[]{:S(2)}) collective-permute-start(bf16[256,512]{0,1:T(8,128)(2,1)} %collective-permute-done.4), channel_id=1, source_target_pairs={{0,1},{1,2},{2,3},{3,4},{4,5},{5,6},{6,7},{7,8},{8,9},{9,10},{10,1... | collective-permute-start | bytes 786440 | tf_op jit(solution)/shard_map/ppermute | solution.py:17
  25.8 0.8 collective-permute-done.1
  26.6 1.9 %collective-permute-start.2 = (bf16[256,512]{1,0:T(8,128)(2,1)S(1)}, bf16[256,512]{1,0:T(8,128)(2,1)S(1)}, u32[]{:S(2)}, u32[]{:S(2)}) collective-permute-start(bf16[256,512]{1,0:T(8,128)(2,1)S(1)} %collective-permute-done.1), channel_id=1, source_target_pairs={{0,1},{1,2},{2,3},{3,4},{4,5},{5,6},{6,7},{7,8},{8,9},{9,10},{10,1... | collective-permute-start | bytes 786440 | tf_op jit(solution)/shard_map/ppermute | solution.py:17
  28.5 1.1 compare_and_fusion
  29.6 0.0 copy-done.5
  29.6 1.2 reshape.106
  30.7 0.2 slice_reduce_fusion.1
  31.0 7.2 %collective-permute-done.2 = bf16[256,512]{1,0:T(8,128)(2,1)S(1)} collective-permute-done((bf16[256,512]{1,0:T(8,128)(2,1)S(1)}, bf16[256,512]{1,0:T(8,128)(2,1)S(1)}, u32[]{:S(2)}, u32[]{:S(2)}) %collective-permute-start.2) | collective-permute-done | bytes 262176 | tf_op jit(solution)/shard_map/ppermute | solution.py:17
  38.2 1.2 pad_maximum_fusion
  39.4 0.5 copy.27
  39.9 0.0 collective-permute-done.5
  39.9 1.2 pad_maximum_fusion.1
  41.2 7.1 %fusion.39 = (f32[4,2,256]{2,1,0:T(2,128)S(1)}, f32[4,2,256,1024]{2,3,1,0:T(8,128)}) fusion(pred[256,1024]{0,1:T(8,128)(4,1)} %compare_and_fusion, bf16[1024,4,128,1]{0,2,3,1:T(8,128)(2,1)S(1)} %bitcast.60, bf16[256,4,2,128]{3,2,1,0:T(2,128)(2,1)} %reshape.106), kind=kOutput, calls=%fused_computation.74 | convolution fusion | flops 545260544 | bytes 10231808 | tf_op jit(solution)/shard_map/sub | solution.py:50
  48.3 5.2 %fusion.7 = f32[4,128,2,256]{3,1,2,0:T(8,128)} fusion(bf16[1024,4,128,1]{0,2,3,1:T(8,128)(2,1)S(1)} %bitcast.59, f32[4,2,256,1024]{2,3,1,0:T(8,128)} %get-tuple-element.18, f32[4,2,256]{2,1,0:T(2,128)S(1)} %get-tuple-element.17), kind=kOutput, calls=%fused_computation.15 | convolution fusion | flops 541589504 | bytes 10493952 | tf_op jit(solution)/shard_map/kgts,skd->tkgd/dot_general | solution.py:52
  53.4 1.6 copy.33
  55.1 0.2 multiply_reduce_fusion.1
  55.3 0.8 convolution_convert_fusion.1
  56.1 0.0 copy-done.1
  56.2 0.3 broadcast_in_dim.12
  56.4 0.2 constant_dynamic-slice_fusion
  56.7 0.0 copy-start.11
  56.7 0.1 collective-permute-start.6
  56.8 0.1 collective-permute-start.7
  56.8 1.8 %collective-permute-start.8 = (bf16[1,128,1024]{2,1,0:T(8,128)(2,1)S(1)}, bf16[1,128,1024]{2,1,0:T(8,128)(2,1)S(1)}, u32[]{:S(2)}, u32[]{:S(2)}) collective-permute-start(bf16[1,128,1024]{2,1,0:T(8,128)(2,1)S(1)} %get-tuple-element.11), channel_id=1, source_target_pairs={{0,3},{1,2},{2,1},{3,0},{4,7},{5,6},{6,5},{7,4},{8,11},{9,10},{10,... | collective-permute-start | bytes 786440 | tf_op jit(solution)/shard_map/ppermute | solution.py:86
  58.6 0.0 collective-permute-start.9
  58.6 2.6 %collective-permute-start.10 = (bf16[1,128,1024]{2,1,0:T(8,128)(2,1)S(1)}, bf16[1,128,1024]{2,1,0:T(8,128)(2,1)S(1)}, u32[]{:S(2)}, u32[]{:S(2)}) collective-permute-start(bf16[1,128,1024]{2,1,0:T(8,128)(2,1)S(1)} %get-tuple-element.9), channel_id=1, source_target_pairs={{0,5},{1,4},{2,7},{3,6},{4,1},{5,0},{6,3},{7,2},{8,13},{9,12},{10,... | collective-permute-start | bytes 786440 | tf_op jit(solution)/shard_map/ppermute | solution.py:86
  61.2 0.0 collective-permute-done.6
  61.2 0.0 collective-permute-start.11
  61.3 8.2 %collective-permute-done.7 = bf16[1,128,1024]{2,1,0:T(8,128)(2,1)S(1)} collective-permute-done((bf16[1,128,1024]{2,1,0:T(8,128)(2,1)S(1)}, bf16[1,128,1024]{2,1,0:T(8,128)(2,1)S(1)}, u32[]{:S(2)}, u32[]{:S(2)}) %collective-permute-start.7) | collective-permute-done | bytes 262176 | tf_op jit(solution)/shard_map/ppermute | solution.py:86
  69.5 0.0 collective-permute-start.12
  69.5 4.5 %collective-permute-done.8 = bf16[1,128,1024]{2,1,0:T(8,128)(2,1)S(1)} collective-permute-done((bf16[1,128,1024]{2,1,0:T(8,128)(2,1)S(1)}, bf16[1,128,1024]{2,1,0:T(8,128)(2,1)S(1)}, u32[]{:S(2)}, u32[]{:S(2)}) %collective-permute-start.8) | collective-permute-done | bytes 262176 | tf_op jit(solution)/shard_map/ppermute | solution.py:86
  74.1 17.1 %collective-permute-done.9 = bf16[1,128,1024]{2,1,0:T(8,128)(2,1)S(1)} collective-permute-done((bf16[1,128,1024]{2,1,0:T(8,128)(2,1)S(1)}, bf16[1,128,1024]{2,1,0:T(8,128)(2,1)S(1)}, u32[]{:S(2)}, u32[]{:S(2)}) %collective-permute-start.9) | collective-permute-done | bytes 262176 | tf_op jit(solution)/shard_map/ppermute | solution.py:86
  91.2 4.4 %collective-permute-done.10 = bf16[1,128,1024]{2,1,0:T(8,128)(2,1)S(1)} collective-permute-done((bf16[1,128,1024]{2,1,0:T(8,128)(2,1)S(1)}, bf16[1,128,1024]{2,1,0:T(8,128)(2,1)S(1)}, u32[]{:S(2)}, u32[]{:S(2)}) %collective-permute-start.10) | collective-permute-done | bytes 262176 | tf_op jit(solution)/shard_map/ppermute | solution.py:86
  95.6 0.0 collective-permute-done.11
  95.7 0.0 collective-permute-done.12
  95.7 0.0 copy-done.11
  95.7 2.6 %fusion.15 = f32[1024,512]{1,0:T(8,128)} fusion(bf16[1024,1024]{1,0:T(8,128)(2,1)S(1)} %bitcast.56, bf16[1,1024,512]{2,1,0:T(8,128)(2,1)S(1)} %copy-done.11), kind=kOutput, calls=%fused_computation.21 | convolution fusion | flops 1073741824 | bytes 5242880 | tf_op jit(solution)/shard_map/dot_general | solution.py:21
  98.3 0.0 copy-done
  98.3 5.6 %convolution_convert_fusion = bf16[1024,1024]{1,0:T(8,128)(2,1)} fusion(f32[1024,512]{1,0:T(8,128)} %fusion.15, bf16[1,512,1024]{2,1,0:T(8,128)(2,1)S(1)} %copy-done, bf16[1024,1024]{1,0:T(8,128)(2,1)S(1)} %bitcast.57, bf16[1,1024,512]{2,1,0:T(8,128)(2,1)} %param.16), kind=kOutput, calls=%fused_computation.12 | convolution fusion | flops 2151677952 | bytes 8388608 | tf_op jit(solution)/shard_map/dot_general | solution.py:24
  103.9 13.2 %all-to-all-start = ((bf16[8,128,1024]{2,1,0:T(8,128)(2,1)}), bf16[8,128,1024]{2,1,0:T(8,128)(2,1)S(1)}, u32[]{:S(2)}, u32[]{:S(2)}) async-start(bf16[8,128,1024]{2,1,0:T(8,128)(2,1)} %bitcast.58), calls=%async_computation | async-start | bytes 4194304 | tf_op jit(solution)/shard_map/all_to_all | solution.py:92
  117.1 0.1 mul.89
  117.3 0.1 copy.34
  117.4 48.7 %all-to-all-done = bf16[8,128,1024]{2,1,0:T(8,128)(2,1)S(1)} async-done(((bf16[8,128,1024]{2,1,0:T(8,128)(2,1)}), bf16[8,128,1024]{2,1,0:T(8,128)(2,1)S(1)}, u32[]{:S(2)}, u32[]{:S(2)}) %all-to-all-start) | async-done | bytes 2097184 | tf_op jit(solution)/shard_map/all_to_all | solution.py:92
  166.2 2.8 %gather_fusion = bf16[512,1024]{1,0:T(8,128)(2,1)} fusion(bf16[1024,1024]{1,0:T(8,128)(2,1)S(1)} %bitcast.54, s32[1024]{0:T(1024)S(1)} %pad_clamp_fusion), kind=kCustom, calls=%fused_computation | custom fusion | bytes 2099200 | tf_op jit(solution)/shard_map/gather | solution.py:94
  168.9 2.4 %reshape.113 = f32[256,2,1024]{2,1,0:T(2,128)S(1)} reshape(bf16[512,1024]{1,0:T(8,128)(2,1)} %gather_fusion) | data formatting | bytes 3145728 | tf_op jit(solution)/shard_map/convert_element_type | solution.py:95
  171.3 0.0 copy-start.4
  171.3 2.6 %multiply_reduce_fusion = f32[256,1024]{1,0:T(8,128)S(1)} fusion(f32[256,2,1024]{2,1,0:T(2,128)S(1)} %reshape.113, f32[256,2]{1,0:T(8,128)S(1)} %copy.34), kind=kLoop, calls=%fused_computation.10 | loop fusion | flops 786432 | bytes 3147776 | tf_op jit(solution)/shard_map/reduce_sum | solution.py:98
  174.0 1.1 add_convert_fusion
  (34 shorter events, 0.3 us)
Async XLA Ops:
  0.0 98.3 %copy-start = (bf16[1,512,1024]{2,1,0:T(8,128)(2,1)S(1)}, bf16[1,512,1024]{2,1,0:T(8,128)(2,1)}, u32[]{:S(2)}) copy-start(bf16[1,512,1024]{2,1,0:T(8,128)(2,1)} %param.17) | copy-start | bytes 3145732
  0.0 29.6 %copy-start.5 = (bf16[256,1024]{1,0:T(8,128)(2,1)S(1)}, bf16[256,1024]{1,0:T(8,128)(2,1)}, u32[]{:S(2)}) copy-start(bf16[256,1024]{1,0:T(8,128)(2,1)} %param.10) | copy-start | bytes 1572868
  1.2 11.3 %collective-permute-start.3 = (bf16[256,512]{0,1:T(8,128)(2,1)S(1)}, bf16[256,512]{0,1:T(8,128)(2,1)S(1)}, u32[]{:S(2)}, u32[]{:S(2)}) collective-permute-start(bf16[256,512]{0,1:T(8,128)(2,1)S(1)} %copy.28), channel_id=1, source_target_pairs={{0,1},{1,2},{2,3},{3,4},{4,5},{5,6},{6,7},{7,8},{8,9},{9,10},{10,1... | collective-permute-start | bytes 786440 | tf_op jit(solution)/shard_map/ppermute | solution.py:17
  3.1 12.2 %collective-permute-start = (bf16[256,512]{1,0:T(8,128)(2,1)}, bf16[256,512]{1,0:T(8,128)(2,1)S(1)}, u32[]{:S(2)}, u32[]{:S(2)}) collective-permute-start(bf16[256,512]{1,0:T(8,128)(2,1)} %param.12), channel_id=1, source_target_pairs={{0,1},{1,2},{2,3},{3,4},{4,5},{5,6},{6,7},{7,8},{8,9},{9,10},{10,1... | collective-permute-start | bytes 786440 | tf_op jit(solution)/shard_map/ppermute | solution.py:17
  12.5 18.4 %copy-start.6 = (bf16[256,512]{0,1:T(8,128)(2,1)}, bf16[256,512]{0,1:T(8,128)(2,1)S(1)}, u32[]{:S(2)}) copy-start(bf16[256,512]{0,1:T(8,128)(2,1)S(1)} %collective-permute-done.3) | copy-start | bytes 786436
  12.5 11.4 %collective-permute-start.4 = (bf16[256,512]{0,1:T(8,128)(2,1)S(1)}, bf16[256,512]{0,1:T(8,128)(2,1)}, u32[]{:S(2)}, u32[]{:S(2)}) collective-permute-start(bf16[256,512]{0,1:T(8,128)(2,1)S(1)} %collective-permute-done.3), channel_id=1, source_target_pairs={{0,1},{1,2},{2,3},{3,4},{4,5},{5,6},{6,7},{7,8},{8,9},{9,10},{10,1... | collective-permute-start | bytes 786440 | tf_op jit(solution)/shard_map/ppermute | solution.py:17
  15.3 15.6 %copy-start.7 = (bf16[256,512]{1,0:T(8,128)(2,1)}, bf16[256,512]{1,0:T(8,128)(2,1)S(1)}, u32[]{:S(2)}) copy-start(bf16[256,512]{1,0:T(8,128)(2,1)S(1)} %collective-permute-done) | copy-start | bytes 786436
  15.3 11.3 %collective-permute-start.1 = (bf16[256,512]{1,0:T(8,128)(2,1)S(1)}, bf16[256,512]{1,0:T(8,128)(2,1)S(1)}, u32[]{:S(2)}, u32[]{:S(2)}) collective-permute-start(bf16[256,512]{1,0:T(8,128)(2,1)S(1)} %collective-permute-done), channel_id=1, source_target_pairs={{0,1},{1,2},{2,3},{3,4},{4,5},{5,6},{6,7},{7,8},{8,9},{9,10},{10,1... | collective-permute-start | bytes 786440 | tf_op jit(solution)/shard_map/ppermute | solution.py:17
  23.9 16.0 %collective-permute-start.5 = (bf16[256,512]{0,1:T(8,128)(2,1)}, bf16[256,512]{0,1:T(8,128)(2,1)}, u32[]{:S(2)}, u32[]{:S(2)}) collective-permute-start(bf16[256,512]{0,1:T(8,128)(2,1)} %collective-permute-done.4), channel_id=1, source_target_pairs={{0,1},{1,2},{2,3},{3,4},{4,5},{5,6},{6,7},{7,8},{8,9},{9,10},{10,1... | collective-permute-start | bytes 786440 | tf_op jit(solution)/shard_map/ppermute | solution.py:17
  26.6 4.4 %copy-start.8 = (bf16[256,512]{1,0:T(8,128)(2,1)}, bf16[256,512]{1,0:T(8,128)(2,1)S(1)}, u32[]{:S(2)}) copy-start(bf16[256,512]{1,0:T(8,128)(2,1)S(1)} %collective-permute-done.1) | copy-start | bytes 786436
  26.6 11.6 %collective-permute-start.2 = (bf16[256,512]{1,0:T(8,128)(2,1)S(1)}, bf16[256,512]{1,0:T(8,128)(2,1)S(1)}, u32[]{:S(2)}, u32[]{:S(2)}) collective-permute-start(bf16[256,512]{1,0:T(8,128)(2,1)S(1)} %collective-permute-done.1), channel_id=1, source_target_pairs={{0,1},{1,2},{2,3},{3,4},{4,5},{5,6},{6,7},{7,8},{8,9},{9,10},{10,1... | collective-permute-start | bytes 786440 | tf_op jit(solution)/shard_map/ppermute | solution.py:17
  53.4 1.6 copy-start.3
  53.4 1.9 %copy-start.9 = (f32[1024]{0:T(1024)S(1)}, f32[1024]{0:T(1024)}, u32[]{:S(2)}) copy-start(f32[1024]{0:T(1024)} %param.14) | copy-start | bytes 12292
  55.1 1.1 copy-start.1
  56.7 39.0 %copy-start.11 = (bf16[1,1024,512]{2,1,0:T(8,128)(2,1)S(1)}, bf16[1,1024,512]{2,1,0:T(8,128)(2,1)}, u32[]{:S(2)}) copy-start(bf16[1,1024,512]{2,1,0:T(8,128)(2,1)} %param.15) | copy-start | bytes 3145732
  56.7 4.5 %collective-permute-start.6 = (bf16[1,128,1024]{2,1,0:T(8,128)(2,1)S(1)}, bf16[1,128,1024]{2,1,0:T(8,128)(2,1)S(1)}, u32[]{:S(2)}, u32[]{:S(2)}) collective-permute-start(bf16[1,128,1024]{2,1,0:T(8,128)(2,1)S(1)} %get-tuple-element.13), channel_id=1, source_target_pairs={{0,1},{1,0},{2,3},{3,2},{4,5},{5,4},{6,7},{7,6},{8,9},{9,8},{10,11... | collective-permute-start | bytes 786440 | tf_op jit(solution)/shard_map/ppermute | solution.py:86
  56.8 12.8 %collective-permute-start.7 = (bf16[1,128,1024]{2,1,0:T(8,128)(2,1)S(1)}, bf16[1,128,1024]{2,1,0:T(8,128)(2,1)S(1)}, u32[]{:S(2)}, u32[]{:S(2)}) collective-permute-start(bf16[1,128,1024]{2,1,0:T(8,128)(2,1)S(1)} %get-tuple-element.12), channel_id=1, source_target_pairs={{0,2},{1,3},{2,0},{3,1},{4,6},{5,7},{6,4},{7,5},{8,10},{9,11},{10,... | collective-permute-start | bytes 786440 | tf_op jit(solution)/shard_map/ppermute | solution.py:86
  56.8 17.2 %collective-permute-start.8 = (bf16[1,128,1024]{2,1,0:T(8,128)(2,1)S(1)}, bf16[1,128,1024]{2,1,0:T(8,128)(2,1)S(1)}, u32[]{:S(2)}, u32[]{:S(2)}) collective-permute-start(bf16[1,128,1024]{2,1,0:T(8,128)(2,1)S(1)} %get-tuple-element.11), channel_id=1, source_target_pairs={{0,3},{1,2},{2,1},{3,0},{4,7},{5,6},{6,5},{7,4},{8,11},{9,10},{10,... | collective-permute-start | bytes 786440 | tf_op jit(solution)/shard_map/ppermute | solution.py:86
  58.6 32.6 %collective-permute-start.9 = (bf16[1,128,1024]{2,1,0:T(8,128)(2,1)S(1)}, bf16[1,128,1024]{2,1,0:T(8,128)(2,1)S(1)}, u32[]{:S(2)}, u32[]{:S(2)}) collective-permute-start(bf16[1,128,1024]{2,1,0:T(8,128)(2,1)S(1)} %get-tuple-element.10), channel_id=1, source_target_pairs={{0,4},{1,5},{2,6},{3,7},{4,0},{5,1},{6,2},{7,3},{8,12},{9,13},{10,... | collective-permute-start | bytes 786440 | tf_op jit(solution)/shard_map/ppermute | solution.py:86
  58.6 37.0 %collective-permute-start.10 = (bf16[1,128,1024]{2,1,0:T(8,128)(2,1)S(1)}, bf16[1,128,1024]{2,1,0:T(8,128)(2,1)S(1)}, u32[]{:S(2)}, u32[]{:S(2)}) collective-permute-start(bf16[1,128,1024]{2,1,0:T(8,128)(2,1)S(1)} %get-tuple-element.9), channel_id=1, source_target_pairs={{0,5},{1,4},{2,7},{3,6},{4,1},{5,0},{6,3},{7,2},{8,13},{9,12},{10,... | collective-permute-start | bytes 786440 | tf_op jit(solution)/shard_map/ppermute | solution.py:86
  61.2 34.4 %collective-permute-start.11 = (bf16[1,128,1024]{2,1,0:T(8,128)(2,1)S(1)}, bf16[1,128,1024]{2,1,0:T(8,128)(2,1)S(1)}, u32[]{:S(2)}, u32[]{:S(2)}) collective-permute-start(bf16[1,128,1024]{2,1,0:T(8,128)(2,1)S(1)} %get-tuple-element.8), channel_id=1, source_target_pairs={{0,6},{1,7},{2,4},{3,5},{4,2},{5,3},{6,0},{7,1},{8,14},{9,15},{10,... | collective-permute-start | bytes 786440 | tf_op jit(solution)/shard_map/ppermute | solution.py:86
  69.5 26.2 %collective-permute-start.12 = (bf16[1,128,1024]{2,1,0:T(8,128)(2,1)S(1)}, bf16[1,128,1024]{2,1,0:T(8,128)(2,1)S(1)}, u32[]{:S(2)}, u32[]{:S(2)}) collective-permute-start(bf16[1,128,1024]{2,1,0:T(8,128)(2,1)S(1)} %get-tuple-element.7), channel_id=1, source_target_pairs={{0,7},{1,6},{2,5},{3,4},{4,3},{5,2},{6,1},{7,0},{8,15},{9,14},{10,... | collective-permute-start | bytes 786440 | tf_op jit(solution)/shard_map/ppermute | solution.py:86
  103.9 13.3 %copy-start.10 = (f32[256,2]{0,1:T(2,128)S(1)}, f32[256,2]{0,1:T(2,128)}, u32[]{:S(2)}) copy-start(f32[256,2]{0,1:T(2,128)} %param.19) | copy-start | bytes 6148
  103.9 62.2 %all-to-all-start = ((bf16[8,128,1024]{2,1,0:T(8,128)(2,1)}), bf16[8,128,1024]{2,1,0:T(8,128)(2,1)S(1)}, u32[]{:S(2)}, u32[]{:S(2)}) async-start(bf16[8,128,1024]{2,1,0:T(8,128)(2,1)} %bitcast.58), calls=%async_computation | async-start | bytes 4194304 | tf_op jit(solution)/shard_map/all_to_all | solution.py:92
  171.3 2.7 %copy-start.2 = (f32[256,1024]{1,0:T(8,128)S(1)}, f32[256,1024]{1,0:T(8,128)}, u32[]{:S(2)}) copy-start(f32[256,1024]{1,0:T(8,128)} %copy-done.1) | copy-start | bytes 3145732
  171.3 2.7 %copy-start.4 = (bf16[256,1024]{1,0:T(8,128)(2,1)S(1)}, bf16[256,1024]{1,0:T(8,128)(2,1)}, u32[]{:S(2)}) copy-start(bf16[256,1024]{1,0:T(8,128)(2,1)} %param.13) | copy-start | bytes 1572868
